TPU v7x, 32 devices: a whole 2x2x4 slice. The times are simulated.
32 devices in a mesh: img: 8 (over z, y), gy: 4 (over x, core).
Axes of the slice: x: 2, y: 2, z: 4, core: 2. Of those that a mesh axis runs over, the one named last changes fastest.
Arguments:
- path: float32 [32, 4, 128, 128], P('img', None, 'gy'), may hold values from -1.2 to 1.2
- start_image: float32 [4, 128, 128], P(None, 'gy'), may hold values from -1.2 to 1.2
- end_image: float32 [4, 128, 128], P(None, 'gy'), may hold values from -1.2 to 1.2
- labels: int32 [4, 128, 128], P(None, 'gy'), may hold values from 0 to 3
- mob_table: float32 [4], replicated, may hold values from 0.2 to 2
Outputs:
- new_path: float32 [32, 4, 128, 128], P('img', None, 'gy')
All inputs are finite; a program needn't handle non-finite values.
Results may differ from a plain program's by a relative error of at most 0.0001.
Values sent between devices are 32-bit elements; how exact they have to be, the bound alone decides.
No kernel may reach another device: no remote copies, remote signals or barrier semaphores. Data moves between devices by JAX's collectives and lax.ppermute only.
A program may use at most 64 MiB of HBM per device.

v0:
```python
import jax
import jax.numpy as jnp
from jax import lax
from jax.sharding import PartitionSpec as P

ITERS = 2
time_step = 0.5
stiffness = 0.25
step_length = 0.05


def extended_2(shard, sides, width):
    for axis, dim in sides:
        size, length = (lax.axis_size(axis), shard.shape[dim])
        up = [(i, (i + 1) % size) for i in range(size - 1)]
        down = [(j, i) for i, j in up]
        last = lax.slice_in_dim(shard, length - width, length, axis=dim)
        initial = lax.slice_in_dim(shard, 0, width, axis=dim)
        before = lax.ppermute(last, axis, up)
        after = lax.ppermute(initial, axis, down)
        shard = jnp.concatenate([before, shard, after], axis=dim)
    return shard


def shifted(block, axis, distance):
    devices = range(lax.axis_size(axis))
    route = [(i - distance, i) for i in devices if i - distance in devices]
    return lax.ppermute(block, axis, route)


def mobility(labels, table):
    result = jnp.zeros(labels.shape, jnp.float32)
    for level in range(table.shape[0]):
        result = result + jnp.where(labels == level, table[level], jnp.float32(0.0))
    return result


def laplace(padded):
    centre = padded[..., 1:-1, :]
    total = jnp.roll(centre, 1, -3) + jnp.roll(centre, -1, -3)
    total = total + jnp.roll(centre, 1, -1) + jnp.roll(centre, -1, -1)
    return total + padded[..., 2:, :] + padded[..., :-2, :] - 6.0 * centre


def drift(padded, mob):
    centre = padded[..., 1:-1, :]
    return mob * (stiffness * laplace(padded) + centre - centre * centre * centre)


def per_device(path, start_image, end_image, labels, mob_table):
    count = path.shape[0]
    groups = lax.axis_size("img")
    images = count * groups
    rank = lax.axis_index("img")
    is_first = rank == 0
    is_final = rank == groups - 1
    gy_count = lax.axis_size("gy")
    rows_here = path.shape[2]
    cells = images * path.shape[1] * rows_here * gy_count * path.shape[3]
    mob = mobility(labels, mob_table)
    for step in range(ITERS):
        extended = jnp.concatenate([start_image[None], path], 0)
        padded = extended_2(extended, (("gy", 2),), 1)
        force = drift(padded, mob)
        current = padded[1 : count + 1, :, 1:-1, :]
        start_part = padded[0, :, 1:-1, :]
        ahead = shifted(current[0], "img", -1)
        ahead = jnp.where(is_final, end_image, ahead)
        later = jnp.concatenate([current[1:], ahead[None]], 0)
        wide_res = (later - current) / time_step - force[1:]
        opening = (current[0] - start_part) / time_step - force[0]
        mres = mob * wide_res
        mpad = extended_2(mres, (("gy", 2),), 1)
        previous = shifted(wide_res[-1], "img", 1)
        previous = jnp.where(is_first, opening, previous)
        earlier = jnp.concatenate([previous[None], wide_res[:-1]], 0)
        adjoint = stiffness * laplace(mpad) + (1.0 - 3.0 * path * path) * mres
        grad = (earlier - wide_res) / time_step - adjoint
        flat = grad.reshape(count, groups, -1)
        columns = lax.all_to_all(flat, "img", split_axis=1, concat_axis=0, tiled=True)
        every = columns.shape[0]
        index = jnp.arange(1, every + 1).astype(jnp.float32)[:, None, None]
        scaled = index * columns
        before_g = jnp.cumsum(columns, 0) - columns
        before_q = jnp.cumsum(scaled, 0) - scaled
        coeff = jnp.sum(columns, 0) - jnp.sum(scaled, 0) / (every + 1)
        solved = time_step * time_step * (index * coeff[None] - index * before_g + before_q)
        back = lax.all_to_all(solved, "img", split_axis=0, concat_axis=1, tiled=True)
        update = back.reshape(grad.shape)
        squares = lax.psum(jnp.sum(update * update), ("img", "gy"))
        scale = step_length * lax.rsqrt(squares / cells + 1e-06)
        path = path - scale * update
    return path


def solution(mesh):
    in_specs = (
        P("img", None, "gy", None),
        P(None, "gy", None),
        P(None, "gy", None),
        P(None, "gy", None),
        P(),
    )
    out_specs = P("img", None, "gy", None)
    return jax.shard_map(
        per_device, mesh=mesh, in_specs=in_specs, out_specs=out_specs, check_vma=False
    )
```

profile of v0, /device:TPU:0, one launch (start us, length us, event | category | flops | bytes accessed | tf_op | source)
XLA Modules:
  0.0 188.7 jit_solution(131051156970023099)
XLA Ops:
  0.0 0.9 fusion.70
  0.9 1.3 collective-permute-start
  2.3 3.2 %collective-permute-start.1 = (f32[5,4,1,128]{3,2,1,0:T(1,128)S(1)}, f32[5,4,1,128]{3,2,1,0:T(1,128)S(1)}, u32[]{:S(2)}, u32[]{:S(2)}) collective-permute-start(f32[5,4,1,128]{3,2,1,0:T(1,128)S(1)} %get-tuple-element.32), channel_id=1, source_target_pairs={{0,1},{1,2},{2,3},{4,5},{5,6},{6,7},{8,9},{9,10},{10,11},{12,13},{... | collective-permute-start | bytes 30728 | tf_op jit(solution)/shard_map/ppermute | solution.py:19
  5.4 1.3 collective-permute-start.2
  8.4 2.5 %select_add_fusion = f32[4,32,128]{2,1,0:T(8,128)S(1)} fusion(s32[4,32,128]{2,1,0:T(8,128)S(1)} %copy-done.6, f32[]{:T(128)} %bitcast.4, f32[]{:T(128)} %bitcast.3, f32[]{:T(128)} %bitcast.2, f32[]{:T(128)} %bitcast.1), kind=kLoop, calls=%fused_computation.139 | loop fusion | flops 180224 | bytes 131088 | tf_op jit(solution)/shard_map/add | solution.py:34
  11.4 1.3 collective-permute-done.2
  13.1 5.3 %collective-permute-start.3 = (f32[4,32,128]{2,1,0:T(8,128)S(1)}, f32[4,32,128]{2,1,0:T(8,128)S(1)}, u32[]{:S(2)}, u32[]{:S(2)}) collective-permute-start(f32[4,32,128]{2,1,0:T(8,128)S(1)} %slice_bitcast_fusion.3), channel_id=1, source_target_pairs={{0,4},{4,8},{8,12},{12,16},{16,20},{20,24},{24,28},{1,5},{5,9},{9,... | collective-permute-start | bytes 196616 | tf_op jit(solution)/shard_map/ppermute | solution.py:28
  18.5 1.3 collective-permute-start.4
  19.8 3.4 %collective-permute-start.5 = (f32[4,4,1,128]{3,2,1,0:T(1,128)S(1)}, f32[4,4,1,128]{3,2,1,0:T(1,128)S(1)}, u32[]{:S(2)}, u32[]{:S(2)}) collective-permute-start(f32[4,4,1,128]{3,2,1,0:T(1,128)S(1)} %get-tuple-element.52), channel_id=1, source_target_pairs={{0,1},{1,2},{2,3},{4,5},{5,6},{6,7},{8,9},{9,10},{10,11},{12,13},{... | collective-permute-start | bytes 24584 | tf_op jit(solution)/shard_map/ppermute | solution.py:19
  23.3 0.8 collective-permute-done.5
  24.5 0.9 copy.6
  25.4 5.7 %all-to-all-start = ((f32[4,8,2048]{2,0,1:T(4,128)}), f32[4,8,2048]{2,0,1:T(4,128)S(1)}, u32[]{:S(2)}, u32[]{:S(2)}) async-start(f32[4,8,2048]{2,0,1:T(4,128)} %copy.6), calls=%async_computation | async-start | bytes 524288 | tf_op jit(solution)/shard_map/all_to_all | solution.py:80
  31.1 9.8 %all-to-all-done = f32[4,8,2048]{2,0,1:T(4,128)S(1)} async-done(((f32[4,8,2048]{2,0,1:T(4,128)}), f32[4,8,2048]{2,0,1:T(4,128)S(1)}, u32[]{:S(2)}, u32[]{:S(2)}) %all-to-all-start) | async-done | bytes 262176 | tf_op jit(solution)/shard_map/all_to_all | solution.py:80
  41.7 0.7 add_multiply_fusion.1
  42.4 13.0 %all_to_all.54 = f32[32,1,2048]{2,1,0:T(1,128)S(1)} all-to-all(f32[32,1,2048]{2,1,0:T(1,128)S(1)} %add_multiply_fusion.1), channel_id=1, replica_groups=mesh['img'=8,'gy'=4] {'img'}, dimensions={0} | all-to-all | bytes 524288 | tf_op jit(solution)/shard_map/all_to_all | solution.py:88
  55.4 1.1 multiply_reduce_fusion.1
  56.6 38.9 %psum.14 = f32[]{:T(128)} all-reduce(f32[]{:T(128)} %multiply_reduce_fusion.1), channel_id=1, replica_groups=mesh['img'=8,'gy'=4] {'img','gy'}, use_global_device_ids=true, to_apply=%region_5.6 | all-reduce | flops 1 | bytes 8 | tf_op jit(solution)/shard_map/psum | solution.py:90
  96.9 1.3 collective-permute-start.6
  98.2 3.0 %collective-permute-start.7 = (f32[5,4,1,128]{3,2,1,0:T(1,128)S(1)}, f32[5,4,1,128]{3,2,1,0:T(1,128)S(1)}, u32[]{:S(2)}, u32[]{:S(2)}) collective-permute-start(f32[5,4,1,128]{3,2,1,0:T(1,128)S(1)} %get-tuple-element.22), channel_id=1, source_target_pairs={{0,1},{1,2},{2,3},{4,5},{5,6},{6,7},{8,9},{9,10},{10,11},{12,13},{... | collective-permute-start | bytes 30728 | tf_op jit(solution)/shard_map/ppermute | solution.py:19
  101.2 1.3 collective-permute-start.8
  103.0 5.1 %collective-permute-done.8 = f32[4,32,128]{2,1,0:T(8,128)S(1)} collective-permute-done((f32[4,32,128]{2,1,0:T(8,128)S(1)}, f32[4,32,128]{2,1,0:T(8,128)S(1)}, u32[]{:S(2)}, u32[]{:S(2)}) %collective-permute-start.8) | collective-permute-done | bytes 65568 | tf_op jit(solution)/shard_map/ppermute | solution.py:28
  108.1 1.0 broadcast_multiply_fusion.2
  109.5 4.7 %collective-permute-start.9 = (f32[4,32,128]{2,1,0:T(8,128)S(1)}, f32[4,32,128]{2,1,0:T(8,128)S(1)}, u32[]{:S(2)}, u32[]{:S(2)}) collective-permute-start(f32[4,32,128]{2,1,0:T(8,128)S(1)} %slice_bitcast_fusion), channel_id=1, source_target_pairs={{0,4},{4,8},{8,12},{12,16},{16,20},{20,24},{24,28},{1,5},{5,9},{9,... | collective-permute-start | bytes 196616 | tf_op jit(solution)/shard_map/ppermute | solution.py:28
  114.3 1.3 collective-permute-start.10
  115.6 3.0 %collective-permute-start.11 = (f32[4,4,1,128]{3,2,1,0:T(1,128)S(1)}, f32[4,4,1,128]{3,2,1,0:T(1,128)S(1)}, u32[]{:S(2)}, u32[]{:S(2)}) collective-permute-start(f32[4,4,1,128]{3,2,1,0:T(1,128)S(1)} %get-tuple-element.42), channel_id=1, source_target_pairs={{0,1},{1,2},{2,3},{4,5},{5,6},{6,7},{8,9},{9,10},{10,11},{12,13},{... | collective-permute-start | bytes 24584 | tf_op jit(solution)/shard_map/ppermute | solution.py:19
  118.7 0.8 collective-permute-done.11
  120.1 12.8 %all_to_all.55 = f32[4,8,2048]{2,0,1:T(4,128)S(1)} all-to-all(f32[4,8,2048]{2,0,1:T(4,128)S(1)} %copy.8), channel_id=1, replica_groups=mesh['img'=8,'gy'=4] {'img'}, dimensions={1} | all-to-all | bytes 524288 | tf_op jit(solution)/shard_map/all_to_all | solution.py:80
  133.6 0.7 add_multiply_fusion
  134.3 12.6 %all_to_all.56 = f32[32,1,2048]{2,1,0:T(1,128)S(1)} all-to-all(f32[32,1,2048]{2,1,0:T(1,128)S(1)} %add_multiply_fusion), channel_id=1, replica_groups=mesh['img'=8,'gy'=4] {'img'}, dimensions={0} | all-to-all | bytes 524288 | tf_op jit(solution)/shard_map/all_to_all | solution.py:88
  147.0 1.1 multiply_reduce_fusion
  148.1 38.9 %psum.15 = f32[]{:T(128)} all-reduce(f32[]{:T(128)} %multiply_reduce_fusion), channel_id=1, replica_groups=mesh['img'=8,'gy'=4] {'img','gy'}, use_global_device_ids=true, to_apply=%region_11.12 | all-reduce | flops 1 | bytes 8 | tf_op jit(solution)/shard_map/psum | solution.py:90
  187.9 0.7 sub.179
  (84 shorter events, 6.8 us)
Async XLA Ops:
  0.0 5.4 %copy-start.2 = (f32[4,4,32,128]{3,2,1,0:T(8,128)S(1)}, f32[4,4,32,128]{3,2,1,0:T(8,128)}, u32[]{:S(2)}) copy-start(f32[4,4,32,128]{3,2,1,0:T(8,128)} %param.5) | copy-start | bytes 786436
  0.9 10.0 %collective-permute-start = (f32[5,4,1,128]{3,2,1,0:T(1,128)S(1)}, f32[5,4,1,128]{3,2,1,0:T(1,128)S(1)}, u32[]{:S(2)}, u32[]{:S(2)}) collective-permute-start(f32[5,4,1,128]{3,2,1,0:T(1,128)S(1)} %get-tuple-element.31), channel_id=1, source_target_pairs={{1,0},{2,1},{3,2},{5,4},{6,5},{7,6},{9,8},{10,9},{11,10},{13,12},{... | collective-permute-start | bytes 30728 | tf_op jit(solution)/shard_map/ppermute | solution.py:20
  2.2 4.5 %copy-start.4 = (f32[4,32,128]{2,1,0:T(8,128)S(1)}, f32[4,32,128]{2,1,0:T(8,128)}, u32[]{:S(2)}) copy-start(f32[4,32,128]{2,1,0:T(8,128)} %param.6) | copy-start | bytes 196612
  2.3 8.7 %collective-permute-start.1 = (f32[5,4,1,128]{3,2,1,0:T(1,128)S(1)}, f32[5,4,1,128]{3,2,1,0:T(1,128)S(1)}, u32[]{:S(2)}, u32[]{:S(2)}) collective-permute-start(f32[5,4,1,128]{3,2,1,0:T(1,128)S(1)} %get-tuple-element.32), channel_id=1, source_target_pairs={{0,1},{1,2},{2,3},{4,5},{5,6},{6,7},{8,9},{9,10},{10,11},{12,13},{... | collective-permute-start | bytes 30728 | tf_op jit(solution)/shard_map/ppermute | solution.py:19
  5.4 7.2 %collective-permute-start.2 = (f32[4,32,128]{2,1,0:T(8,128)S(1)}, f32[4,32,128]{2,1,0:T(8,128)S(1)}, u32[]{:S(2)}, u32[]{:S(2)}) collective-permute-start(f32[4,32,128]{2,1,0:T(8,128)S(1)} %slice_bitcast_fusion.5), channel_id=1, source_target_pairs={{4,0},{8,4},{12,8},{16,12},{20,16},{24,20},{28,24},{5,1},{9,5},{13... | collective-permute-start | bytes 196616 | tf_op jit(solution)/shard_map/ppermute | solution.py:28
  7.1 0.7 copy-start.7
  7.1 1.3 copy-start.6
  10.9 1.7 copy-start.5
  10.9 1.7 copy-start.3
  11.3 1.3 slice-start.1
  13.1 10.1 %collective-permute-start.3 = (f32[4,32,128]{2,1,0:T(8,128)S(1)}, f32[4,32,128]{2,1,0:T(8,128)S(1)}, u32[]{:S(2)}, u32[]{:S(2)}) collective-permute-start(f32[4,32,128]{2,1,0:T(8,128)S(1)} %slice_bitcast_fusion.3), channel_id=1, source_target_pairs={{0,4},{4,8},{8,12},{12,16},{16,20},{20,24},{24,28},{1,5},{5,9},{9,... | collective-permute-start | bytes 196616 | tf_op jit(solution)/shard_map/ppermute | solution.py:28
  18.5 4.8 %collective-permute-start.4 = (f32[4,4,1,128]{3,2,1,0:T(1,128)S(1)}, f32[4,4,1,128]{3,2,1,0:T(1,128)S(1)}, u32[]{:S(2)}, u32[]{:S(2)}) collective-permute-start(f32[4,4,1,128]{3,2,1,0:T(1,128)S(1)} %get-tuple-element.51), channel_id=1, source_target_pairs={{1,0},{2,1},{3,2},{5,4},{6,5},{7,6},{9,8},{10,9},{11,10},{13,12},{... | collective-permute-start | bytes 24584 | tf_op jit(solution)/shard_map/ppermute | solution.py:20
  19.8 4.2 %collective-permute-start.5 = (f32[4,4,1,128]{3,2,1,0:T(1,128)S(1)}, f32[4,4,1,128]{3,2,1,0:T(1,128)S(1)}, u32[]{:S(2)}, u32[]{:S(2)}) collective-permute-start(f32[4,4,1,128]{3,2,1,0:T(1,128)S(1)} %get-tuple-element.52), channel_id=1, source_target_pairs={{0,1},{1,2},{2,3},{4,5},{5,6},{6,7},{8,9},{9,10},{10,11},{12,13},{... | collective-permute-start | bytes 24584 | tf_op jit(solution)/shard_map/ppermute | solution.py:19
  25.4 15.6 %all-to-all-start = ((f32[4,8,2048]{2,0,1:T(4,128)}), f32[4,8,2048]{2,0,1:T(4,128)S(1)}, u32[]{:S(2)}, u32[]{:S(2)}) async-start(f32[4,8,2048]{2,0,1:T(4,128)} %copy.6), calls=%async_computation | async-start | bytes 524288 | tf_op jit(solution)/shard_map/all_to_all | solution.py:80
  96.5 6.1 %copy-start = (f32[4,4,32,128]{3,2,1,0:T(8,128)}, f32[4,4,32,128]{3,2,1,0:T(8,128)S(1)}, u32[]{:S(2)}) copy-start(f32[4,4,32,128]{3,2,1,0:T(8,128)S(1)} %sub.164) | copy-start | bytes 786436
  96.9 5.7 %collective-permute-start.6 = (f32[5,4,1,128]{3,2,1,0:T(1,128)S(1)}, f32[5,4,1,128]{3,2,1,0:T(1,128)S(1)}, u32[]{:S(2)}, u32[]{:S(2)}) collective-permute-start(f32[5,4,1,128]{3,2,1,0:T(1,128)S(1)} %get-tuple-element.21), channel_id=1, source_target_pairs={{1,0},{2,1},{3,2},{5,4},{6,5},{7,6},{9,8},{10,9},{11,10},{13,12},{... | collective-permute-start | bytes 30728 | tf_op jit(solution)/shard_map/ppermute | solution.py:20
  98.2 4.4 %collective-permute-start.7 = (f32[5,4,1,128]{3,2,1,0:T(1,128)S(1)}, f32[5,4,1,128]{3,2,1,0:T(1,128)S(1)}, u32[]{:S(2)}, u32[]{:S(2)}) collective-permute-start(f32[5,4,1,128]{3,2,1,0:T(1,128)S(1)} %get-tuple-element.22), channel_id=1, source_target_pairs={{0,1},{1,2},{2,3},{4,5},{5,6},{6,7},{8,9},{9,10},{10,11},{12,13},{... | collective-permute-start | bytes 30728 | tf_op jit(solution)/shard_map/ppermute | solution.py:19
  101.2 6.8 %collective-permute-start.8 = (f32[4,32,128]{2,1,0:T(8,128)S(1)}, f32[4,32,128]{2,1,0:T(8,128)S(1)}, u32[]{:S(2)}, u32[]{:S(2)}) collective-permute-start(f32[4,32,128]{2,1,0:T(8,128)S(1)} %slice_bitcast_fusion.2), channel_id=1, source_target_pairs={{4,0},{8,4},{12,8},{16,12},{20,16},{24,20},{28,24},{5,1},{9,5},{13... | collective-permute-start | bytes 196616 | tf_op jit(solution)/shard_map/ppermute | solution.py:28
  103.0 5.1 %slice-start = ((f32[4,4,32,128]{3,2,1,0:T(8,128)}), f32[3,4,32,128]{3,2,1,0:T(8,128)S(1)}, s32[]{:S(2)}) async-start(f32[4,4,32,128]{3,2,1,0:T(8,128)} %copy-done), calls=%async_computation.4 | async-start | bytes 393216 | tf_op jit(solution)/shard_map/slice | solution.py:69
  109.5 9.2 %copy-start.1 = (f32[4,4,32,128]{3,2,1,0:T(8,128)S(1)}, f32[4,4,32,128]{3,2,1,0:T(8,128)}, u32[]{:S(2)}) copy-start(f32[4,4,32,128]{3,2,1,0:T(8,128)} %copy-done) | copy-start | bytes 786436
  109.5 9.1 %collective-permute-start.9 = (f32[4,32,128]{2,1,0:T(8,128)S(1)}, f32[4,32,128]{2,1,0:T(8,128)S(1)}, u32[]{:S(2)}, u32[]{:S(2)}) collective-permute-start(f32[4,32,128]{2,1,0:T(8,128)S(1)} %slice_bitcast_fusion), channel_id=1, source_target_pairs={{0,4},{4,8},{8,12},{12,16},{16,20},{20,24},{24,28},{1,5},{5,9},{9,... | collective-permute-start | bytes 196616 | tf_op jit(solution)/shard_map/ppermute | solution.py:28
  114.3 4.4 %collective-permute-start.10 = (f32[4,4,1,128]{3,2,1,0:T(1,128)S(1)}, f32[4,4,1,128]{3,2,1,0:T(1,128)S(1)}, u32[]{:S(2)}, u32[]{:S(2)}) collective-permute-start(f32[4,4,1,128]{3,2,1,0:T(1,128)S(1)} %get-tuple-element.41), channel_id=1, source_target_pairs={{1,0},{2,1},{3,2},{5,4},{6,5},{7,6},{9,8},{10,9},{11,10},{13,12},{... | collective-permute-start | bytes 24584 | tf_op jit(solution)/shard_map/ppermute | solution.py:20
  115.6 3.8 %collective-permute-start.11 = (f32[4,4,1,128]{3,2,1,0:T(1,128)S(1)}, f32[4,4,1,128]{3,2,1,0:T(1,128)S(1)}, u32[]{:S(2)}, u32[]{:S(2)}) collective-permute-start(f32[4,4,1,128]{3,2,1,0:T(1,128)S(1)} %get-tuple-element.42), channel_id=1, source_target_pairs={{0,1},{1,2},{2,3},{4,5},{5,6},{6,7},{8,9},{9,10},{10,11},{12,13},{... | collective-permute-start | bytes 24584 | tf_op jit(solution)/shard_map/ppermute | solution.py:19
where the time goes:
time: 190 us; the launch traced here: 189 us
  blocking collectives  116 us (61%)
  starting transfers between devices  36.1 us (19%)
  waiting for transfers between devices  17.7 us (9%)
  other arithmetic  12.6 us (7%)
  local copies, waits for them, and re-layouts  3.91 us (2%)
  between operations  2.03 us (1%)
    psum x2, blocking collectives, per_device(): squares = lax.psum(jnp.sum(update * update), ('img', 'gy'))  77.8 us
    all_to_all x2, blocking collectives, per_device(): lax.all_to_all(solved, 'img', split_axis=0, concat_axis=1, tiled=True)  25.7 us
    all_to_all x1, blocking collectives, per_device(): lax.all_to_all(flat, 'img', split_axis=1, concat_axis=0, tiled=True)  12.8 us
    ppermute x4, starting transfers between devices, extended_2(): before = lax.ppermute(last, axis, up)  12.6 us
    ppermute x4, starting transfers between devices, shifted(): return lax.ppermute(block, axis, route)  12.6 us
    all_to_all x1, waiting for transfers between devices, per_device(): lax.all_to_all(flat, 'img', split_axis=1, concat_axis=0, tiled=True)  9.83 us
    ppermute x4, waiting for transfers between devices, shifted(): return lax.ppermute(block, axis, route)  6.37 us
    all_to_all x1, starting transfers between devices, per_device(): lax.all_to_all(flat, 'img', split_axis=1, concat_axis=0, tiled=True)  5.72 us
  transfers between devices with their start and end apart: 13, of which 5 were waited for; matrix products, arithmetic and copies ran while one was open for 2% of the time, Pallas kernels for 0%

commit v1 on v0

--- a/solution.py
+++ b/solution.py
@@ -85,7 +85,10 @@
         before_q = jnp.cumsum(scaled, 0) - scaled
         coeff = jnp.sum(columns, 0) - jnp.sum(scaled, 0) / (every + 1)
         solved = time_step * time_step * (index * coeff[None] - index * before_g + before_q)
-        back = lax.all_to_all(solved, "img", split_axis=0, concat_axis=1, tiled=True)
+        n_dev = lax.axis_size("img")
+        pieces = jnp.stack(jnp.split(solved, n_dev, axis=0), axis=0)
+        pieces = lax.all_to_all(pieces, "img", split_axis=0, concat_axis=0)
+        back = jnp.concatenate(pieces, axis=1)
         update = back.reshape(grad.shape)
         squares = lax.psum(jnp.sum(update * update), ("img", "gy"))
         scale = step_length * lax.rsqrt(squares / cells + 1e-06)

time: 190 us -> 190 us (level)
  no operation moved by 1% of the time
where the time goes in v1:
time: 190 us; the launch traced here: 189 us
  blocking collectives  116 us (61%)
  starting transfers between devices  36.1 us (19%)
  waiting for transfers between devices  17.7 us (9%)
  other arithmetic  12.9 us (7%)
  local copies, waits for them, and re-layouts  4.07 us (2%)
  between operations  2.11 us (1%)
    psum x2, blocking collectives, per_device(): squares = lax.psum(jnp.sum(update * update), ('img', 'gy'))  77.8 us
    all_to_all x2, blocking collectives, per_device(): pieces = lax.all_to_all(pieces, 'img', split_axis=0, concat_axis=0)  25.7 us
    all_to_all x1, blocking collectives, per_device(): lax.all_to_all(flat, 'img', split_axis=1, concat_axis=0, tiled=True)  12.8 us
    ppermute x4, starting transfers between devices, extended_2(): before = lax.ppermute(last, axis, up)  12.6 us
    ppermute x4, starting transfers between devices, shifted(): return lax.ppermute(block, axis, route)  12.6 us
    all_to_all x1, waiting for transfers between devices, per_device(): lax.all_to_all(flat, 'img', split_axis=1, concat_axis=0, tiled=True)  9.83 us
    ppermute x4, waiting for transfers between devices, shifted(): return lax.ppermute(block, axis, route)  6.37 us
    all_to_all x1, starting transfers between devices, per_device(): lax.all_to_all(flat, 'img', split_axis=1, concat_axis=0, tiled=True)  5.72 us
  transfers between devices with their start and end apart: 13, of which 5 were waited for; matrix products, arithmetic and copies ran while one was open for 2% of the time, Pallas kernels for 0%

profile of v1, /device:TPU:0, one launch (start us, length us, event | category | flops | bytes accessed | tf_op | source)
XLA Modules:
  0.0 189.3 jit_solution(7907299605925975271)
XLA Ops:
  0.0 0.9 fusion.70
  0.9 1.3 collective-permute-start
  2.3 3.2 %collective-permute-start.1 = (f32[5,4,1,128]{3,2,1,0:T(1,128)S(1)}, f32[5,4,1,128]{3,2,1,0:T(1,128)S(1)}, u32[]{:S(2)}, u32[]{:S(2)}) collective-permute-start(f32[5,4,1,128]{3,2,1,0:T(1,128)S(1)} %get-tuple-element.32), channel_id=1, source_target_pairs={{0,1},{1,2},{2,3},{4,5},{5,6},{6,7},{8,9},{9,10},{10,11},{12,13},{... | collective-permute-start | bytes 30728 | tf_op jit(solution)/shard_map/ppermute | solution.py:19
  5.4 1.3 collective-permute-start.2
  8.4 2.5 %select_add_fusion = f32[4,32,128]{2,1,0:T(8,128)S(1)} fusion(s32[4,32,128]{2,1,0:T(8,128)S(1)} %copy-done.6, f32[]{:T(128)} %bitcast.4, f32[]{:T(128)} %bitcast.3, f32[]{:T(128)} %bitcast.2, f32[]{:T(128)} %bitcast.1), kind=kLoop, calls=%fused_computation.139 | loop fusion | flops 180224 | bytes 131088 | tf_op jit(solution)/shard_map/add | solution.py:34
  11.4 1.3 collective-permute-done.2
  13.1 5.3 %collective-permute-start.3 = (f32[4,32,128]{2,1,0:T(8,128)S(1)}, f32[4,32,128]{2,1,0:T(8,128)S(1)}, u32[]{:S(2)}, u32[]{:S(2)}) collective-permute-start(f32[4,32,128]{2,1,0:T(8,128)S(1)} %slice_bitcast_fusion.3), channel_id=1, source_target_pairs={{0,4},{4,8},{8,12},{12,16},{16,20},{20,24},{24,28},{1,5},{5,9},{9,... | collective-permute-start | bytes 196616 | tf_op jit(solution)/shard_map/ppermute | solution.py:28
  18.5 1.3 collective-permute-start.4
  19.8 3.4 %collective-permute-start.5 = (f32[4,4,1,128]{3,2,1,0:T(1,128)S(1)}, f32[4,4,1,128]{3,2,1,0:T(1,128)S(1)}, u32[]{:S(2)}, u32[]{:S(2)}) collective-permute-start(f32[4,4,1,128]{3,2,1,0:T(1,128)S(1)} %get-tuple-element.52), channel_id=1, source_target_pairs={{0,1},{1,2},{2,3},{4,5},{5,6},{6,7},{8,9},{9,10},{10,11},{12,13},{... | collective-permute-start | bytes 24584 | tf_op jit(solution)/shard_map/ppermute | solution.py:19
  23.3 0.8 collective-permute-done.5
  24.5 0.9 copy.8
  25.4 5.7 %all-to-all-start = ((f32[4,8,2048]{2,0,1:T(4,128)}), f32[4,8,2048]{2,0,1:T(4,128)S(1)}, u32[]{:S(2)}, u32[]{:S(2)}) async-start(f32[4,8,2048]{2,0,1:T(4,128)} %copy.8), calls=%async_computation | async-start | bytes 524288 | tf_op jit(solution)/shard_map/all_to_all | solution.py:80
  31.1 9.8 %all-to-all-done = f32[4,8,2048]{2,0,1:T(4,128)S(1)} async-done(((f32[4,8,2048]{2,0,1:T(4,128)}), f32[4,8,2048]{2,0,1:T(4,128)S(1)}, u32[]{:S(2)}, u32[]{:S(2)}) %all-to-all-start) | async-done | bytes 262176 | tf_op jit(solution)/shard_map/all_to_all | solution.py:80
  41.7 0.7 add_multiply_fusion.1
  42.5 13.0 %all_to_all.46 = f32[8,4,1,2048]{3,2,1,0:T(1,128)S(1)} all-to-all(f32[8,4,1,2048]{3,2,1,0:T(1,128)S(1)} %constant_dynamic-update-slice_fusion), channel_id=1, replica_groups=mesh['img'=8,'gy'=4] {'img'}, dimensions={0} | all-to-all | bytes 524288 | tf_op jit(solution)/shard_map/all_to_all | solution.py:90
  55.5 1.1 multiply_reduce_fusion.1
  56.7 38.9 %psum.14 = f32[]{:T(128)} all-reduce(f32[]{:T(128)} %multiply_reduce_fusion.1), channel_id=1, replica_groups=mesh['img'=8,'gy'=4] {'img','gy'}, use_global_device_ids=true, to_apply=%region_5.6 | all-reduce | flops 1 | bytes 8 | tf_op jit(solution)/shard_map/psum | solution.py:93
  97.2 1.3 collective-permute-start.6
  98.5 3.0 %collective-permute-start.7 = (f32[5,4,1,128]{3,2,1,0:T(1,128)S(1)}, f32[5,4,1,128]{3,2,1,0:T(1,128)S(1)}, u32[]{:S(2)}, u32[]{:S(2)}) collective-permute-start(f32[5,4,1,128]{3,2,1,0:T(1,128)S(1)} %get-tuple-element.22), channel_id=1, source_target_pairs={{0,1},{1,2},{2,3},{4,5},{5,6},{6,7},{8,9},{9,10},{10,11},{12,13},{... | collective-permute-start | bytes 30728 | tf_op jit(solution)/shard_map/ppermute | solution.py:19
  101.5 1.3 collective-permute-start.8
  103.3 5.1 %collective-permute-done.8 = f32[4,32,128]{2,1,0:T(8,128)S(1)} collective-permute-done((f32[4,32,128]{2,1,0:T(8,128)S(1)}, f32[4,32,128]{2,1,0:T(8,128)S(1)}, u32[]{:S(2)}, u32[]{:S(2)}) %collective-permute-start.8) | collective-permute-done | bytes 65568 | tf_op jit(solution)/shard_map/ppermute | solution.py:28
  108.4 1.0 broadcast_multiply_fusion
  109.8 4.7 %collective-permute-start.9 = (f32[4,32,128]{2,1,0:T(8,128)S(1)}, f32[4,32,128]{2,1,0:T(8,128)S(1)}, u32[]{:S(2)}, u32[]{:S(2)}) collective-permute-start(f32[4,32,128]{2,1,0:T(8,128)S(1)} %slice_bitcast_fusion), channel_id=1, source_target_pairs={{0,4},{4,8},{8,12},{12,16},{16,20},{20,24},{24,28},{1,5},{5,9},{9,... | collective-permute-start | bytes 196616 | tf_op jit(solution)/shard_map/ppermute | solution.py:28
  114.6 1.3 collective-permute-start.10
  115.9 3.0 %collective-permute-start.11 = (f32[4,4,1,128]{3,2,1,0:T(1,128)S(1)}, f32[4,4,1,128]{3,2,1,0:T(1,128)S(1)}, u32[]{:S(2)}, u32[]{:S(2)}) collective-permute-start(f32[4,4,1,128]{3,2,1,0:T(1,128)S(1)} %get-tuple-element.42), channel_id=1, source_target_pairs={{0,1},{1,2},{2,3},{4,5},{5,6},{6,7},{8,9},{9,10},{10,11},{12,13},{... | collective-permute-start | bytes 24584 | tf_op jit(solution)/shard_map/ppermute | solution.py:19
  119.0 0.8 collective-permute-done.11
  120.3 12.8 %all_to_all.47 = f32[4,8,2048]{2,0,1:T(4,128)S(1)} all-to-all(f32[4,8,2048]{2,0,1:T(4,128)S(1)} %copy.10), channel_id=1, replica_groups=mesh['img'=8,'gy'=4] {'img'}, dimensions={1} | all-to-all | bytes 524288 | tf_op jit(solution)/shard_map/all_to_all | solution.py:80
  133.9 0.7 add_multiply_fusion
  134.7 12.6 %all_to_all.48 = f32[8,4,1,2048]{3,2,1,0:T(1,128)S(1)} all-to-all(f32[8,4,1,2048]{3,2,1,0:T(1,128)S(1)} %constant_dynamic-update-slice_fusion.8), channel_id=1, replica_groups=mesh['img'=8,'gy'=4] {'img'}, dimensions={0} | all-to-all | bytes 524288 | tf_op jit(solution)/shard_map/all_to_all | solution.py:90
  147.4 1.1 multiply_reduce_fusion
  148.5 38.9 %psum.15 = f32[]{:T(128)} all-reduce(f32[]{:T(128)} %multiply_reduce_fusion), channel_id=1, replica_groups=mesh['img'=8,'gy'=4] {'img','gy'}, use_global_device_ids=true, to_apply=%region_11.12 | all-reduce | flops 1 | bytes 8 | tf_op jit(solution)/shard_map/psum | solution.py:93
  188.5 0.7 sub.179
  (100 shorter events, 7.3 us)
Async XLA Ops:
  0.0 5.4 %copy-start.2 = (f32[4,4,32,128]{3,2,1,0:T(8,128)S(1)}, f32[4,4,32,128]{3,2,1,0:T(8,128)}, u32[]{:S(2)}) copy-start(f32[4,4,32,128]{3,2,1,0:T(8,128)} %param.5) | copy-start | bytes 786436
  0.9 10.0 %collective-permute-start = (f32[5,4,1,128]{3,2,1,0:T(1,128)S(1)}, f32[5,4,1,128]{3,2,1,0:T(1,128)S(1)}, u32[]{:S(2)}, u32[]{:S(2)}) collective-permute-start(f32[5,4,1,128]{3,2,1,0:T(1,128)S(1)} %get-tuple-element.31), channel_id=1, source_target_pairs={{1,0},{2,1},{3,2},{5,4},{6,5},{7,6},{9,8},{10,9},{11,10},{13,12},{... | collective-permute-start | bytes 30728 | tf_op jit(solution)/shard_map/ppermute | solution.py:20
  2.2 4.5 %copy-start.4 = (f32[4,32,128]{2,1,0:T(8,128)S(1)}, f32[4,32,128]{2,1,0:T(8,128)}, u32[]{:S(2)}) copy-start(f32[4,32,128]{2,1,0:T(8,128)} %param.6) | copy-start | bytes 196612
  2.3 8.7 %collective-permute-start.1 = (f32[5,4,1,128]{3,2,1,0:T(1,128)S(1)}, f32[5,4,1,128]{3,2,1,0:T(1,128)S(1)}, u32[]{:S(2)}, u32[]{:S(2)}) collective-permute-start(f32[5,4,1,128]{3,2,1,0:T(1,128)S(1)} %get-tuple-element.32), channel_id=1, source_target_pairs={{0,1},{1,2},{2,3},{4,5},{5,6},{6,7},{8,9},{9,10},{10,11},{12,13},{... | collective-permute-start | bytes 30728 | tf_op jit(solution)/shard_map/ppermute | solution.py:19
  5.4 7.2 %collective-permute-start.2 = (f32[4,32,128]{2,1,0:T(8,128)S(1)}, f32[4,32,128]{2,1,0:T(8,128)S(1)}, u32[]{:S(2)}, u32[]{:S(2)}) collective-permute-start(f32[4,32,128]{2,1,0:T(8,128)S(1)} %slice_bitcast_fusion.5), channel_id=1, source_target_pairs={{4,0},{8,4},{12,8},{16,12},{20,16},{24,20},{28,24},{5,1},{9,5},{13... | collective-permute-start | bytes 196616 | tf_op jit(solution)/shard_map/ppermute | solution.py:28
  7.1 0.7 copy-start.7
  7.1 1.3 copy-start.6
  10.9 1.7 copy-start.5
  10.9 1.7 copy-start.3
  11.3 1.3 slice-start.1
  13.1 10.1 %collective-permute-start.3 = (f32[4,32,128]{2,1,0:T(8,128)S(1)}, f32[4,32,128]{2,1,0:T(8,128)S(1)}, u32[]{:S(2)}, u32[]{:S(2)}) collective-permute-start(f32[4,32,128]{2,1,0:T(8,128)S(1)} %slice_bitcast_fusion.3), channel_id=1, source_target_pairs={{0,4},{4,8},{8,12},{12,16},{16,20},{20,24},{24,28},{1,5},{5,9},{9,... | collective-permute-start | bytes 196616 | tf_op jit(solution)/shard_map/ppermute | solution.py:28
  18.5 4.8 %collective-permute-start.4 = (f32[4,4,1,128]{3,2,1,0:T(1,128)S(1)}, f32[4,4,1,128]{3,2,1,0:T(1,128)S(1)}, u32[]{:S(2)}, u32[]{:S(2)}) collective-permute-start(f32[4,4,1,128]{3,2,1,0:T(1,128)S(1)} %get-tuple-element.51), channel_id=1, source_target_pairs={{1,0},{2,1},{3,2},{5,4},{6,5},{7,6},{9,8},{10,9},{11,10},{13,12},{... | collective-permute-start | bytes 24584 | tf_op jit(solution)/shard_map/ppermute | solution.py:20
  19.8 4.2 %collective-permute-start.5 = (f32[4,4,1,128]{3,2,1,0:T(1,128)S(1)}, f32[4,4,1,128]{3,2,1,0:T(1,128)S(1)}, u32[]{:S(2)}, u32[]{:S(2)}) collective-permute-start(f32[4,4,1,128]{3,2,1,0:T(1,128)S(1)} %get-tuple-element.52), channel_id=1, source_target_pairs={{0,1},{1,2},{2,3},{4,5},{5,6},{6,7},{8,9},{9,10},{10,11},{12,13},{... | collective-permute-start | bytes 24584 | tf_op jit(solution)/shard_map/ppermute | solution.py:19
  25.4 15.6 %all-to-all-start = ((f32[4,8,2048]{2,0,1:T(4,128)}), f32[4,8,2048]{2,0,1:T(4,128)S(1)}, u32[]{:S(2)}, u32[]{:S(2)}) async-start(f32[4,8,2048]{2,0,1:T(4,128)} %copy.8), calls=%async_computation | async-start | bytes 524288 | tf_op jit(solution)/shard_map/all_to_all | solution.py:80
  96.7 6.1 %copy-start = (f32[4,4,32,128]{3,2,1,0:T(8,128)}, f32[4,4,32,128]{3,2,1,0:T(8,128)S(1)}, u32[]{:S(2)}) copy-start(f32[4,4,32,128]{3,2,1,0:T(8,128)S(1)} %sub.164) | copy-start | bytes 786436
  97.2 5.7 %collective-permute-start.6 = (f32[5,4,1,128]{3,2,1,0:T(1,128)S(1)}, f32[5,4,1,128]{3,2,1,0:T(1,128)S(1)}, u32[]{:S(2)}, u32[]{:S(2)}) collective-permute-start(f32[5,4,1,128]{3,2,1,0:T(1,128)S(1)} %get-tuple-element.21), channel_id=1, source_target_pairs={{1,0},{2,1},{3,2},{5,4},{6,5},{7,6},{9,8},{10,9},{11,10},{13,12},{... | collective-permute-start | bytes 30728 | tf_op jit(solution)/shard_map/ppermute | solution.py:20
  98.5 4.4 %collective-permute-start.7 = (f32[5,4,1,128]{3,2,1,0:T(1,128)S(1)}, f32[5,4,1,128]{3,2,1,0:T(1,128)S(1)}, u32[]{:S(2)}, u32[]{:S(2)}) collective-permute-start(f32[5,4,1,128]{3,2,1,0:T(1,128)S(1)} %get-tuple-element.22), channel_id=1, source_target_pairs={{0,1},{1,2},{2,3},{4,5},{5,6},{6,7},{8,9},{9,10},{10,11},{12,13},{... | collective-permute-start | bytes 30728 | tf_op jit(solution)/shard_map/ppermute | solution.py:19
  101.5 6.8 %collective-permute-start.8 = (f32[4,32,128]{2,1,0:T(8,128)S(1)}, f32[4,32,128]{2,1,0:T(8,128)S(1)}, u32[]{:S(2)}, u32[]{:S(2)}) collective-permute-start(f32[4,32,128]{2,1,0:T(8,128)S(1)} %slice_bitcast_fusion.2), channel_id=1, source_target_pairs={{4,0},{8,4},{12,8},{16,12},{20,16},{24,20},{28,24},{5,1},{9,5},{13... | collective-permute-start | bytes 196616 | tf_op jit(solution)/shard_map/ppermute | solution.py:28
  103.3 5.1 %slice-start = ((f32[4,4,32,128]{3,2,1,0:T(8,128)}), f32[3,4,32,128]{3,2,1,0:T(8,128)S(1)}, s32[]{:S(2)}) async-start(f32[4,4,32,128]{3,2,1,0:T(8,128)} %copy-done), calls=%async_computation.4 | async-start | bytes 393216 | tf_op jit(solution)/shard_map/slice | solution.py:69
  109.8 9.2 %copy-start.1 = (f32[4,4,32,128]{3,2,1,0:T(8,128)S(1)}, f32[4,4,32,128]{3,2,1,0:T(8,128)}, u32[]{:S(2)}) copy-start(f32[4,4,32,128]{3,2,1,0:T(8,128)} %copy-done) | copy-start | bytes 786436
  109.8 9.1 %collective-permute-start.9 = (f32[4,32,128]{2,1,0:T(8,128)S(1)}, f32[4,32,128]{2,1,0:T(8,128)S(1)}, u32[]{:S(2)}, u32[]{:S(2)}) collective-permute-start(f32[4,32,128]{2,1,0:T(8,128)S(1)} %slice_bitcast_fusion), channel_id=1, source_target_pairs={{0,4},{4,8},{8,12},{12,16},{16,20},{20,24},{24,28},{1,5},{5,9},{9,... | collective-permute-start | bytes 196616 | tf_op jit(solution)/shard_map/ppermute | solution.py:28
  114.6 4.4 %collective-permute-start.10 = (f32[4,4,1,128]{3,2,1,0:T(1,128)S(1)}, f32[4,4,1,128]{3,2,1,0:T(1,128)S(1)}, u32[]{:S(2)}, u32[]{:S(2)}) collective-permute-start(f32[4,4,1,128]{3,2,1,0:T(1,128)S(1)} %get-tuple-element.41), channel_id=1, source_target_pairs={{1,0},{2,1},{3,2},{5,4},{6,5},{7,6},{9,8},{10,9},{11,10},{13,12},{... | collective-permute-start | bytes 24584 | tf_op jit(solution)/shard_map/ppermute | solution.py:20
  115.9 3.8 %collective-permute-start.11 = (f32[4,4,1,128]{3,2,1,0:T(1,128)S(1)}, f32[4,4,1,128]{3,2,1,0:T(1,128)S(1)}, u32[]{:S(2)}, u32[]{:S(2)}) collective-permute-start(f32[4,4,1,128]{3,2,1,0:T(1,128)S(1)} %get-tuple-element.42), channel_id=1, source_target_pairs={{0,1},{1,2},{2,3},{4,5},{5,6},{6,7},{8,9},{9,10},{10,11},{12,13},{... | collective-permute-start | bytes 24584 | tf_op jit(solution)/shard_map/ppermute | solution.py:19
